TPU v7x, 32 devices: a whole 2x2x4 slice. The times are simulated.
32 devices in a mesh: dp: 2 (over y), expert: 16 (over z, x, core).
Axes of the slice: x: 2, y: 2, z: 4, core: 2. Of those that a mesh axis runs over, the one named last changes fastest.
Arguments:
- soft_tokens: bfloat16 [2048, 2048], P('expert', 'dp'), may hold values from -6 to 6
- expert_ids: int32 [2048, 8], P('expert'), may hold values from 0 to 31, all different within a row; in each aligned block of 128 rows (0 to 127, 128 to 255, ...) at most 40 rows name the same one
- gate_mix: float32 [2048, 8], P('expert'), may hold values from 0.05 to 0.35
- w_gate: bfloat16 [32, 2048, 768], P('expert', 'dp'), may hold values from -0.125 to 0.125
- w_up: bfloat16 [32, 2048, 768], P('expert', 'dp'), may hold values from -0.125 to 0.125
- w_down: bfloat16 [32, 768, 2048], P('expert', None, 'dp'), may hold values from -0.21875 to 0.21875
- out_grad: bfloat16 [2048, 2048], P('expert', 'dp'), may hold values from -6 to 6
Outputs:
- mixed: bfloat16 [2048, 2048], P('expert', 'dp')
- token_grad: bfloat16 [2048, 2048], P('expert', 'dp')
Inputs may be any that keep to these rules, and one draw needn't show every extreme that they name: `expert_ids`: each row names 8 different experts. Among the 128 rows of one device no expert is named by more than 40 rows, and in some device one expert is named by exactly 40 rows.
All inputs are finite; a program needn't handle non-finite values.
Results may differ from a plain program's by a relative error of at most 0.023.
Values may be sent and summed in bfloat16 or wider, within the bound.
A program may use at most 128 MiB of HBM per device.

v0:
```python
import jax
import jax.numpy as jnp
from jax import lax
from jax.sharding import PartitionSpec as P


def slot_table(expert_ids, experts, capacity):
    tok_rows, top_count = expert_ids.shape
    flat_count = tok_rows * top_count
    flat_ids = expert_ids.reshape(flat_count)
    onehot = (flat_ids[:, None] == jnp.arange(experts, dtype=jnp.int32)[None, :]).astype(jnp.int32)
    before = jnp.sum(jnp.cumsum(onehot, axis=0) * onehot, axis=1) - 1
    position = flat_ids * capacity + before
    source = jnp.full((experts * capacity,), flat_count, jnp.int32)
    source = source.at[position].set(jnp.arange(flat_count, dtype=jnp.int32))
    return (position, source)


def place_rows(values, source, top_count):
    tok_rows = values.shape[0]
    valid = source < tok_rows * top_count
    token = jnp.minimum(source // top_count, tok_rows - 1)
    return jnp.where(valid[:, None], values[token], jnp.zeros((), values.dtype))


def activate(sums, hidden):
    gate_part = sums[..., :hidden]
    upper_part = sums[..., hidden:]
    sigmoid_gate = jax.nn.sigmoid(gate_part)
    return (gate_part * sigmoid_gate * upper_part).astype(jnp.bfloat16)


def act_grad(sums, back, hidden):
    gate_part = sums[..., :hidden]
    upper_part = sums[..., hidden:]
    sigmoid_gate = jax.nn.sigmoid(gate_part)
    d_gate = back * upper_part * sigmoid_gate * (1.0 + gate_part * (1.0 - sigmoid_gate))
    d_upper = back * gate_part * sigmoid_gate
    return jnp.concatenate([d_gate, d_upper], axis=-1).astype(jnp.bfloat16)


def combine(returned, position, gate_mix):
    tok_rows, top_count = gate_mix.shape
    flat_rows = returned.reshape(-1, returned.shape[-1])
    picked = flat_rows[position].reshape(tok_rows, top_count, -1).astype(jnp.float32)
    return jnp.sum(gate_mix[:, :, None] * picked, axis=1).astype(jnp.bfloat16)


def per_device(soft_tokens, expert_ids, gate_mix, w_gate, w_up, w_down, out_grad):
    tok_rows, width_part = soft_tokens.shape
    top_count = expert_ids.shape[1]
    local_experts = w_gate.shape[0]
    hidden = w_gate.shape[2]
    groups = lax.axis_size("expert")
    experts = groups * local_experts
    capacity = max(2, tok_rows * top_count * 5 // (4 * experts))
    position, source = slot_table(expert_ids, experts, capacity)
    w_both = jnp.concatenate([w_gate, w_up], axis=2)
    layout = (groups, local_experts, capacity, width_part)
    token_rows = place_rows(soft_tokens, source, top_count).reshape(layout)
    grad_rows_out = place_rows(out_grad, source, top_count).reshape(layout)
    token_recv = lax.all_to_all(token_rows, "expert", split_axis=0, concat_axis=0, tiled=True)
    dp_count = lax.axis_size("dp")
    share = groups // dp_count
    first_row = lax.axis_index("dp") * share
    piece = token_recv
    own_sums = lax.psum_scatter(
        jnp.einsum("secd,edf->secf", piece, w_both, preferred_element_type=jnp.float32).astype(
            jnp.bfloat16
        ),
        "dp",
        scatter_dimension=0,
        tiled=True,
    ).astype(jnp.float32)
    hidden_act = lax.all_gather(activate(own_sums, hidden), "dp", axis=0, tiled=True)
    expert_out = jnp.einsum(
        "secf,efd->secd", hidden_act, w_down, preferred_element_type=jnp.float32
    ).astype(jnp.bfloat16)
    out_returned = lax.all_to_all(expert_out, "expert", split_axis=0, concat_axis=0, tiled=True)
    grad_recv = lax.all_to_all(grad_rows_out, "expert", split_axis=0, concat_axis=0, tiled=True)
    piece = grad_recv
    whole_back = lax.psum(
        jnp.einsum("secd,efd->secf", piece, w_down, preferred_element_type=jnp.float32).astype(
            jnp.bfloat16
        ),
        "dp",
    ).astype(jnp.float32)
    own_back = lax.dynamic_slice_in_dim(whole_back, first_row, share, 0)
    dpre = lax.all_gather(act_grad(own_sums, own_back, hidden), "dp", axis=0, tiled=True)
    grad_rows = jnp.einsum(
        "secf,edf->secd", dpre, w_both, preferred_element_type=jnp.float32
    ).astype(jnp.bfloat16)
    grad_returned = lax.all_to_all(grad_rows, "expert", split_axis=0, concat_axis=0, tiled=True)
    mixed = combine(out_returned, position, gate_mix)
    token_grad = combine(grad_returned, position, gate_mix)
    return (mixed, token_grad)


def solution(mesh):
    in_specs = (
        P("expert", "dp"),
        P("expert", None),
        P("expert", None),
        P("expert", "dp", None),
        P("expert", "dp", None),
        P("expert", None, "dp"),
        P("expert", "dp"),
    )
    out_specs = (P("expert", "dp"), P("expert", "dp"))
    return jax.shard_map(
        per_device, mesh=mesh, in_specs=in_specs, out_specs=out_specs, check_vma=False
    )
```

profile of v0, /device:TPU:11, one launch (start us, length us, event | category | flops | bytes accessed | tf_op | source)
XLA Modules:
  0.0 453.7 jit_solution(9259662578411656731)
XLA Ops:
  7.2 1.0 copy.23
  9.0 1.3 broadcast_multiply_fusion
  10.9 15.7 %reduce-window.6 = s32[32,8,128]{2,1,0:T(8,128)S(1)} reduce-window(s32[32,8,128]{2,1,0:T(8,128)} %fusion.23, s32[]{:T(128)} %constant.19.clone.1), window={size=1x1x128 pad=0_0x0_0x127_0}, to_apply=%region_0.0 | reduce-window | flops 4161536 | bytes 262148 | tf_op jit(solution)/shard_map/reduce-window
  27.4 1.0 copy.25
  31.5 4.3 scatter_custom_fusion
  35.9 5.1 %gather_fusion.2 = bf16[1280,1024]{1,0:T(8,128)(2,1)} fusion(bf16[128,1024]{1,0:T(8,128)(2,1)S(1)} %copy-done.1, s32[2048]{0:T(1024)S(1)} %pad_clamp_fusion), kind=kCustom, calls=%fused_computation.2 | custom fusion | bytes 5248000 | tf_op jit(solution)/shard_map/gather | solution.py:23
  41.0 7.7 %gather_fusion = bf16[1280,1024]{1,0:T(8,128)(2,1)} fusion(bf16[128,1024]{1,0:T(8,128)(2,1)} %param.7, s32[2048]{0:T(1024)S(1)} %pad_clamp_fusion), kind=kCustom, calls=%fused_computation | custom fusion | bytes 5248000 | tf_op jit(solution)/shard_map/gather | solution.py:23
  48.8 3.9 broadcast_select_fusion
  52.7 64.9 %all_to_all.20 = bf16[16,2,40,1024]{3,2,1,0:T(8,128)(2,1)} all-to-all(bf16[16,2,40,1024]{3,2,1,0:T(8,128)(2,1)S(1)} %get-tuple-element.8), channel_id=1, replica_groups=mesh['dp'=2,'expert'=16] {'expert'}, dimensions={0} | all-to-all | bytes 5242880 | tf_op jit(solution)/shard_map/all_to_all | solution.py:62
  117.6 9.7 %fusion.3 = bf16[16,2,40,1536]{3,2,0,1:T(8,128)(2,1)} fusion(bf16[2,1024,768]{2,1,0:T(8,128)(2,1)} %param.11, bf16[2,1024,768]{2,1,0:T(8,128)(2,1)} %param.10, bf16[16,2,40,1024]{3,2,1,0:T(8,128)(2,1)} %all_to_all.20), kind=kOutput, calls=%fused_computation.12 | convolution fusion | flops 4041080832 | bytes 12845056 | tf_op jit(solution)/shard_map/secd,edf->secf/dot_general | solution.py:68
  127.3 2.6 copy.33
  129.9 4.0 copy.36
  134.0 63.6 %all_to_all.21 = bf16[16,2,40,1024]{3,2,1,0:T(8,128)(2,1)S(1)} all-to-all(bf16[16,2,40,1024]{3,2,1,0:T(8,128)(2,1)} %get-tuple-element.7), channel_id=1, replica_groups=mesh['dp'=2,'expert'=16] {'expert'}, dimensions={0} | all-to-all | bytes 5242880 | tf_op jit(solution)/shard_map/all_to_all | solution.py:80
  197.6 3.6 convert_bitcast_fusion.2
  201.3 2.1 copy.37
  203.4 2.4 copy_convert_fusion
  205.8 55.2 %all-reduce.2.cloned.1.call-done = bf16[16,2,40,768]{3,2,0,1:T(8,128)(2,1)} async-done(((bf16[16,2,40,768]{3,2,0,1:T(8,128)(2,1)}), bf16[16,2,40,768]{3,2,0,1:T(8,128)(2,1)}) %all-reduce.2.cloned.1.call-update) | async-done | bytes 1966096 | tf_op jit(solution)/shard_map/psum | solution.py:82
  261.1 5.1 %fusion.16 = (bf16[8,2,40,768]{3,2,0,1:T(8,128)(2,1)}, bf16[8,2,40,768]{3,2,0,1:T(8,128)(2,1)}, bf16[8,2,40,768]{3,2,0,1:T(8,128)(2,1)}) fusion(f32[8,2,40,1536]{3,2,0,1:T(8,128)} %copy_convert_fusion, bf16[16,2,40,768]{3,2,0,1:T(8,128)(2,1)} %all-reduce.2.cloned.1.call-done, s32[]{:T(128)S(6)} %select_n.39), kind=kLoop, calls=%fused_computation.29 | loop fusion | flops 8355840 | bytes 7864324 | tf_op jit(solution)/shard_map/convert.2
  266.3 3.0 pad_maximum_fusion
  269.2 28.7 %all-gather.3.cloned.1.call-done = bf16[16,2,40,768]{3,2,0,1:T(8,128)(2,1)} async-done(((bf16[8,2,40,768]{3,2,0,1:T(8,128)(2,1)}), bf16[16,2,40,768]{3,2,0,1:T(8,128)(2,1)}) %all-gather.3.cloned.1.call-update) | async-done | bytes 1966096 | tf_op jit(solution)/shard_map/all_gather | solution.py:75
  298.0 3.8 convert_bitcast_fusion.1
  301.7 1.8 copy.28
  303.6 6.5 %all-to-all-start.1 = ((bf16[16,2,40,1024]{3,2,1,0:T(8,128)(2,1)}), bf16[16,2,40,1024]{3,2,1,0:T(8,128)(2,1)}, u32[]{:S(2)}, u32[]{:S(2)}) async-start(bf16[16,2,40,1024]{3,2,1,0:T(8,128)(2,1)} %copy.28), calls=%async_computation.1 | async-start | bytes 5242880 | tf_op jit(solution)/shard_map/all_to_all | solution.py:79
  310.1 43.1 %all-gather.5.cloned.1.call-done = bf16[16,2,40,1536]{3,2,0,1:T(8,128)(2,1)} async-done(((bf16[8,2,40,1536]{3,2,0,1:T(8,128)(2,1)}), bf16[16,2,40,1536]{3,2,0,1:T(8,128)(2,1)}) %all-gather.5.cloned.1.call-update) | async-done | bytes 3932176 | tf_op jit(solution)/shard_map/all_gather | solution.py:89
  353.2 8.3 %convert_bitcast_fusion = bf16[16,2,40,1024]{3,2,0,1:T(8,128)(2,1)S(1)} fusion(bf16[16,2,40,1536]{3,2,0,1:T(8,128)(2,1)} %all-gather.5.cloned.1.call-done, bf16[2,1024,768]{2,1,0:T(8,128)(2,1)} %param.11, bf16[2,1024,768]{2,1,0:T(8,128)(2,1)} %param.10), kind=kOutput, calls=%fused_computation.19 | convolution fusion | flops 4040425472 | bytes 12845056 | tf_op jit(solution)/shard_map/secf,edf->secd/dot_general | solution.py:90
  361.5 1.8 copy.30
  363.3 5.5 %all-to-all-done.1 = bf16[16,2,40,1024]{3,2,1,0:T(8,128)(2,1)} async-done(((bf16[16,2,40,1024]{3,2,1,0:T(8,128)(2,1)}), bf16[16,2,40,1024]{3,2,1,0:T(8,128)(2,1)}, u32[]{:S(2)}, u32[]{:S(2)}) %all-to-all-start.1) | async-done | bytes 2621472 | tf_op jit(solution)/shard_map/all_to_all | solution.py:79
  368.8 4.8 %all-to-all-start.3 = ((bf16[16,2,40,1024]{3,2,1,0:T(8,128)(2,1)}), bf16[16,2,40,1024]{3,2,1,0:T(8,128)(2,1)}, u32[]{:S(2)}, u32[]{:S(2)}) async-start(bf16[16,2,40,1024]{3,2,1,0:T(8,128)(2,1)} %copy.30), calls=%async_computation.3 | async-start | bytes 5242880 | tf_op jit(solution)/shard_map/all_to_all | solution.py:93
  373.7 8.1 %gather_fusion.1 = bf16[1024,1024]{1,0:T(8,128)(2,1)} fusion(bf16[1280,1024]{1,0:T(8,128)(2,1)} %bitcast.11, s32[1024]{0:T(1024)S(1)} %broadcast_clamp_fusion), kind=kCustom, calls=%fused_computation.1 | custom fusion | bytes 4198400 | tf_op jit(solution)/shard_map/gather | solution.py:45
  381.9 50.5 %all-to-all-done.3 = bf16[16,2,40,1024]{3,2,1,0:T(8,128)(2,1)} async-done(((bf16[16,2,40,1024]{3,2,1,0:T(8,128)(2,1)}), bf16[16,2,40,1024]{3,2,1,0:T(8,128)(2,1)}, u32[]{:S(2)}, u32[]{:S(2)}) %all-to-all-start.3) | async-done | bytes 2621472 | tf_op jit(solution)/shard_map/all_to_all | solution.py:93
  432.4 8.1 %gather_fusion.3 = bf16[1024,1024]{1,0:T(8,128)(2,1)} fusion(bf16[1280,1024]{1,0:T(8,128)(2,1)} %bitcast.18, s32[1024]{0:T(1024)S(1)} %broadcast_clamp_fusion), kind=kCustom, calls=%fused_computation.3 | custom fusion | bytes 4198400 | tf_op jit(solution)/shard_map/gather | solution.py:45
  440.5 6.7 %fusion = (bf16[128,1024]{1,0:T(8,128)(2,1)}, bf16[128,1024]{1,0:T(8,128)(2,1)}) fusion(bf16[1024,1024]{1,0:T(8,128)(2,1)} %gather_fusion.3, f32[128,8]{1,0:T(8,128)S(1)} %copy.21, bf16[1024,1024]{1,0:T(8,128)(2,1)} %gather_fusion.1), kind=kLoop, calls=%fused_computation.7 | loop fusion | flops 6029312 | bytes 4722688 | tf_op jit(solution)/shard_map/reduce_sum | solution.py:46
  (35 shorter events, 5.8 us)
Async XLA Ops:
  7.2 190.4 %copy-start = (bf16[2,768,1024]{2,1,0:T(8,128)(2,1)S(1)}, bf16[2,768,1024]{2,1,0:T(8,128)(2,1)}, u32[]{:S(2)}) copy-start(bf16[2,768,1024]{2,1,0:T(8,128)(2,1)} %param.12) | copy-start | bytes 9437188
  7.2 28.7 %copy-start.1 = (bf16[128,1024]{1,0:T(8,128)(2,1)S(1)}, bf16[128,1024]{1,0:T(8,128)(2,1)}, u32[]{:S(2)}) copy-start(bf16[128,1024]{1,0:T(8,128)(2,1)} %param.13) | copy-start | bytes 786436
  7.2 194.1 %reduce-scatter.5.cloned.1.call-start = ((), (), s32[]{:S(2)}) async-start(), calls=%async_computation.8 | async-start | bytes 5898240
  134.0 127.1 %all-reduce.2.cloned.1.call-start = ((), (), s32[]{:S(2)}) async-start(), calls=%async_computation.6 | async-start | bytes 3932160 | tf_op jit(solution)/shard_map/psum | solution.py:82
  201.2 96.7 %all-gather.3.cloned.1.call-start = ((), (), s32[]{:S(2)}) async-start(), calls=%async_computation.5 | async-start | bytes 2949120 | tf_op jit(solution)/shard_map/all_gather | solution.py:75
  266.2 87.0 %all-gather.5.cloned.1.call-start = ((), (), s32[]{:S(2)}) async-start(), calls=%async_computation.7 | async-start | bytes 5898240 | tf_op jit(solution)/shard_map/all_gather | solution.py:89
  303.6 65.3 %all-to-all-start.1 = ((bf16[16,2,40,1024]{3,2,1,0:T(8,128)(2,1)}), bf16[16,2,40,1024]{3,2,1,0:T(8,128)(2,1)}, u32[]{:S(2)}, u32[]{:S(2)}) async-start(bf16[16,2,40,1024]{3,2,1,0:T(8,128)(2,1)} %copy.28), calls=%async_computation.1 | async-start | bytes 5242880 | tf_op jit(solution)/shard_map/all_to_all | solution.py:79
  363.3 10.3 %copy-start.2 = (f32[128,8]{0,1:T(8,128)S(1)}, f32[128,8]{0,1:T(8,128)}, u32[]{:S(2)}) copy-start(f32[128,8]{0,1:T(8,128)} %param.9) | copy-start | bytes 12292
  368.8 63.5 %all-to-all-start.3 = ((bf16[16,2,40,1024]{3,2,1,0:T(8,128)(2,1)}), bf16[16,2,40,1024]{3,2,1,0:T(8,128)(2,1)}, u32[]{:S(2)}, u32[]{:S(2)}) async-start(bf16[16,2,40,1024]{3,2,1,0:T(8,128)(2,1)} %copy.30), calls=%async_computation.3 | async-start | bytes 5242880 | tf_op jit(solution)/shard_map/all_to_all | solution.py:93
Sparse Core Ops, SparseCore 0:
  134.1 51.6 reduce-scatter.4
  201.4 59.6 all-reduce.1
  266.3 31.6 all-gather.2
  299.4 53.7 all-gather.4
where the time goes:
time: 455 us; the launch traced here: 454 us
  waiting for transfers between devices  183 us (40%)
  blocking collectives  129 us (28%)
  local copies, waits for them, and re-layouts  51.8 us (11%)
  other arithmetic  39.5 us (9%)
  matrix products  25.4 us (6%)
  between operations  13.9 us (3%)
  starting transfers between devices  11.4 us (3%)
    all_to_all x1, blocking collectives, per_device(): lax.all_to_all(token_rows, 'expert', split_axis=0, concat_axis=0, tiled=T...  64.9 us
    all_to_all x1, blocking collectives, per_device(): lax.all_to_all(grad_rows_out, 'expert', split_axis=0, concat_axis=0, tile...  63.6 us
    psum x1, waiting for transfers between devices, per_device(): lax.psum(jnp.einsum('secd,efd->secf', piece, w_down, preferred_element_ty...  55.2 us
    all_to_all x1, waiting for transfers between devices, per_device(): lax.all_to_all(grad_rows, 'expert', split_axis=0, concat_axis=0, tiled=True)  50.5 us
    all_gather x1, waiting for transfers between devices, per_device(): lax.all_gather(act_grad(own_sums, own_back, hidden), 'dp', axis=0, tiled=...  43.1 us
    all_gather x1, waiting for transfers between devices, per_device(): lax.all_gather(activate(own_sums, hidden), 'dp', axis=0, tiled=True)  28.7 us
    another operation x4, other arithmetic  20.9 us
    gather x2, local copies, waits for them, and re-layouts, combine(): flat_rows[position].reshape(tok_rows, top_count, -1).astype(jnp.float32)  16.3 us
  transfers between devices with their start and end apart: 6, of which 5 were waited for; matrix products, arithmetic and copies ran while one was open for 8% of the time, Pallas kernels for 0%

commit v1 on v0

--- a/solution.py
+++ b/solution.py
@@ -2,6 +2,18 @@
 import jax.numpy as jnp
 from jax import lax
 from jax.sharding import PartitionSpec as P
+
+
+def cut_along(x, dim, length):
+    lengths = x.shape
+    blocks = x.reshape(*lengths[:dim], length, lengths[dim] // length, *lengths[dim + 1 :])
+    return jnp.moveaxis(blocks, dim, 0)
+
+
+def laid_out(blocks, dim):
+    shape = list(blocks.shape[1:])
+    shape[dim] *= blocks.shape[0]
+    return jnp.moveaxis(blocks, 0, dim).reshape(shape)
 
 
 def slot_table(expert_ids, experts, capacity):
@@ -77,7 +89,14 @@
         "secf,efd->secd", hidden_act, w_down, preferred_element_type=jnp.float32
     ).astype(jnp.bfloat16)
     out_returned = lax.all_to_all(expert_out, "expert", split_axis=0, concat_axis=0, tiled=True)
-    grad_recv = lax.all_to_all(grad_rows_out, "expert", split_axis=0, concat_axis=0, tiled=True)
+    peers, place = (lax.axis_size("expert"), lax.axis_index("expert"))
+    blocks = cut_along(grad_rows_out, 0, peers)
+    outs = [blocks[place]]
+    for step in range(1, peers):
+        sent = blocks[place ^ step]
+        outs.append(lax.ppermute(sent, "expert", [(i, i ^ step) for i in range(peers)]))
+    blocks = jnp.stack(outs)[place ^ jnp.arange(peers)]
+    grad_recv = laid_out(blocks, 0)
     piece = grad_recv
     whole_back = lax.psum(
         jnp.einsum("secd,efd->secf", piece, w_down, preferred_element_type=jnp.float32).astype(

time: 455 us -> 467 us (1.026)
  blocking collectives: 129 us -> 64.9 us
  waiting for transfers between devices: 183 us -> 227 us
  starting transfers between devices: 11.4 us -> 27 us
  local copies, waits for them, and re-layouts: 51.8 us -> 64.8 us
    all_to_all x1 -> x0, blocking collectives: 63.6 us -> none  [per_device(): lax.all_to_all(grad_rows_out, 'expert', split_axis=0, concat_axis=0, tile...]
    ppermute x0 -> x15, waiting for transfers between devices: none -> 44.1 us  [per_device(): lax.ppermute(sent, 'expert', [(i, i ^ step) for i in range(peers)])]
    ppermute x0 -> x15, starting transfers between devices: none -> 15.4 us  [per_device(): lax.ppermute(sent, 'expert', [(i, i ^ step) for i in range(peers)])]
    unnamed x11 -> x27, local copies, waits for them, and re-layouts: 9.83 us -> 19.9 us
  transfers between devices with their start and end apart: 6 -> 21, of which waited for: 5 -> 15; matrix products, arithmetic and copies ran while one was open for 8% -> 13% of each run, Pallas kernels for 0% -> 0%
where the time goes in v1:
time: 467 us; the launch traced here: 465 us
  waiting for transfers between devices  227 us (49%)
  blocking collectives  64.9 us (14%)
  local copies, waits for them, and re-layouts  64.8 us (14%)
  other arithmetic  40.4 us (9%)
  matrix products  27.1 us (6%)
  starting transfers between devices  27 us (6%)
  between operations  14 us (3%)
    all_to_all x1, blocking collectives, per_device(): lax.all_to_all(token_rows, 'expert', split_axis=0, concat_axis=0, tiled=T...  64.9 us
    psum x1, waiting for transfers between devices, per_device(): lax.psum(jnp.einsum('secd,efd->secf', piece, w_down, preferred_element_ty...  54.9 us
    all_to_all x1, waiting for transfers between devices, per_device(): lax.all_to_all(grad_rows, 'expert', split_axis=0, concat_axis=0, tiled=True)  50.5 us
    ppermute x15, waiting for transfers between devices, per_device(): lax.ppermute(sent, 'expert', [(i, i ^ step) for i in range(peers)])  44.1 us
    all_gather x1, waiting for transfers between devices, per_device(): lax.all_gather(act_grad(own_sums, own_back, hidden), 'dp', axis=0, tiled=...  43.1 us
    all_gather x1, waiting for transfers between devices, per_device(): lax.all_gather(activate(own_sums, hidden), 'dp', axis=0, tiled=True)  28.7 us
    another operation x4, other arithmetic  20.9 us
    unnamed x27, local copies, waits for them, and re-layouts  19.9 us
  transfers between devices with their start and end apart: 21, of which 15 were waited for; matrix products, arithmetic and copies ran while one was open for 13% of the time, Pallas kernels for 0%

profile of v1, /device:TPU:11, one launch (start us, length us, event | category | flops | bytes accessed | tf_op | source)
XLA Modules:
  0.0 465.2 jit_solution(1795450855280467373)
XLA Ops:
  10.9 15.7 %reduce-window.6 = s32[32,8,128]{2,1,0:T(8,128)S(1)} reduce-window(s32[32,8,128]{2,1,0:T(8,128)} %fusion.23, s32[]{:T(128)} %constant.31.clone.1), window={size=1x1x128 pad=0_0x0_0x127_0}, to_apply=%region_0.0 | reduce-window | flops 4161536 | bytes 262148 | tf_op jit(solution)/shard_map/reduce-window
  31.5 4.3 scatter_custom_fusion
  36.0 5.1 %gather_fusion = bf16[1280,1024]{1,0:T(8,128)(2,1)} fusion(bf16[128,1024]{1,0:T(8,128)(2,1)S(1)} %copy-done.1, s32[2048]{0:T(1024)S(1)} %pad_clamp_fusion), kind=kCustom, calls=%fused_computation | custom fusion | bytes 5248000 | tf_op jit(solution)/shard_map/gather | solution.py:35
  43.1 64.9 %all_to_all.15 = bf16[16,2,40,1024]{3,2,1,0:T(8,128)(2,1)} all-to-all(bf16[16,2,40,1024]{3,2,1,0:T(8,128)(2,1)S(1)} %broadcast_select_fusion.1), channel_id=1, replica_groups=mesh['dp'=2,'expert'=16] {'expert'}, dimensions={0} | all-to-all | bytes 5242880 | tf_op jit(solution)/shard_map/all_to_all | solution.py:74
  108.0 9.7 %fusion.3 = bf16[16,2,40,1536]{3,2,0,1:T(8,128)(2,1)} fusion(bf16[2,1024,768]{2,1,0:T(8,128)(2,1)} %param.11, bf16[2,1024,768]{2,1,0:T(8,128)(2,1)} %param.10, bf16[16,2,40,1024]{3,2,1,0:T(8,128)(2,1)} %all_to_all.15), kind=kOutput, calls=%fused_computation.13 | convolution fusion | flops 4041080832 | bytes 12845056 | tf_op jit(solution)/shard_map/secd,edf->secf/dot_general | solution.py:80
  120.3 4.0 copy.37
  125.3 5.1 %gather_fusion.2 = bf16[1280,1024]{1,0:T(8,128)(2,1)} fusion(bf16[128,1024]{1,0:T(8,128)(2,1)S(1)} %copy-done.2, s32[2048]{0:T(1024)S(1)} %pad_clamp_fusion), kind=kCustom, calls=%fused_computation.2 | custom fusion | bytes 5248000 | tf_op jit(solution)/shard_map/gather | solution.py:35
  130.4 2.8 broadcast_select_fusion
  149.1 4.7 %collective-permute-done.5 = bf16[1,2,40,1024]{3,2,1,0:T(8,128)(2,1)S(1)} collective-permute-done((bf16[1,2,40,1024]{3,2,1,0:T(8,128)(2,1)S(1)}, bf16[1,2,40,1024]{3,2,1,0:T(8,128)(2,1)S(1)}, u32[]{:S(2)}, u32[]{:S(2)}) %collective-permute-start.5) | collective-permute-done | bytes 163872 | tf_op jit(solution)/shard_map/ppermute | solution.py:97
  153.8 4.9 %collective-permute-start.10 = (bf16[1,2,40,1024]{3,2,1,0:T(8,128)(2,1)S(1)}, bf16[1,2,40,1024]{3,2,1,0:T(8,128)(2,1)S(1)}, u32[]{:S(2)}, u32[]{:S(2)}) collective-permute-start(bf16[1,2,40,1024]{3,2,1,0:T(8,128)(2,1)S(1)} %get-tuple-element.11), channel_id=1, source_target_pairs={{0,11},{1,10},{2,9},{3,8},{4,15},{5,14},{6,13},{7,12},{8,3},{9,2},... | collective-permute-start | bytes 491528 | tf_op jit(solution)/shard_map/ppermute | solution.py:97
  162.1 11.6 %collective-permute-done.8 = bf16[1,2,40,1024]{3,2,1,0:T(8,128)(2,1)S(1)} collective-permute-done((bf16[1,2,40,1024]{3,2,1,0:T(8,128)(2,1)S(1)}, bf16[1,2,40,1024]{3,2,1,0:T(8,128)(2,1)S(1)}, u32[]{:S(2)}, u32[]{:S(2)}) %collective-permute-start.8) | collective-permute-done | bytes 163872 | tf_op jit(solution)/shard_map/ppermute | solution.py:97
  174.4 6.3 %collective-permute-done.9 = bf16[1,2,40,1024]{3,2,1,0:T(8,128)(2,1)S(1)} collective-permute-done((bf16[1,2,40,1024]{3,2,1,0:T(8,128)(2,1)S(1)}, bf16[1,2,40,1024]{3,2,1,0:T(8,128)(2,1)S(1)}, u32[]{:S(2)}, u32[]{:S(2)}) %collective-permute-start.9) | collective-permute-done | bytes 163872 | tf_op jit(solution)/shard_map/ppermute | solution.py:97
  181.4 4.7 %collective-permute-done.10 = bf16[1,2,40,1024]{3,2,1,0:T(8,128)(2,1)S(1)} collective-permute-done((bf16[1,2,40,1024]{3,2,1,0:T(8,128)(2,1)S(1)}, bf16[1,2,40,1024]{3,2,1,0:T(8,128)(2,1)S(1)}, u32[]{:S(2)}, u32[]{:S(2)}) %collective-permute-start.10) | collective-permute-done | bytes 163872 | tf_op jit(solution)/shard_map/ppermute | solution.py:97
  186.8 5.3 %collective-permute-done.11 = bf16[1,2,40,1024]{3,2,1,0:T(8,128)(2,1)S(1)} collective-permute-done((bf16[1,2,40,1024]{3,2,1,0:T(8,128)(2,1)S(1)}, bf16[1,2,40,1024]{3,2,1,0:T(8,128)(2,1)S(1)}, u32[]{:S(2)}, u32[]{:S(2)}) %collective-permute-start.11) | collective-permute-done | bytes 163872 | tf_op jit(solution)/shard_map/ppermute | solution.py:97
  196.1 3.5 collective-permute-done.13
  200.3 2.8 collective-permute-done.14
  203.8 4.0 gather_fusion.3
  207.8 5.3 %convert_bitcast_fusion.2 = bf16[16,2,40,768]{3,2,0,1:T(8,128)(2,1)} fusion(bf16[2,768,1024]{2,1,0:T(8,128)(2,1)S(1)} %copy-done, bf16[16,2,40,1024]{3,2,1,0:T(8,128)(2,1)} %gather_fusion.3), kind=kOutput, calls=%fused_computation.33 | convolution fusion | flops 2014248960 | bytes 7733248 | tf_op jit(solution)/shard_map/secd,efd->secf/dot_general | solution.py:102
  217.7 54.9 %all-reduce.2.cloned.1.call-done = bf16[16,2,40,768]{3,2,0,1:T(8,128)(2,1)} async-done(((bf16[16,2,40,768]{3,2,0,1:T(8,128)(2,1)}), bf16[16,2,40,768]{3,2,0,1:T(8,128)(2,1)}) %all-reduce.2.cloned.1.call-update) | async-done | bytes 1966096 | tf_op jit(solution)/shard_map/psum | solution.py:101
  272.6 5.1 %fusion.16 = (bf16[8,2,40,768]{3,2,0,1:T(8,128)(2,1)}, bf16[8,2,40,768]{3,2,0,1:T(8,128)(2,1)}, bf16[8,2,40,768]{3,2,0,1:T(8,128)(2,1)}) fusion(f32[8,2,40,1536]{3,2,0,1:T(8,128)} %copy_convert_fusion, bf16[16,2,40,768]{3,2,0,1:T(8,128)(2,1)} %all-reduce.2.cloned.1.call-done, s32[]{:T(128)S(6)} %select_n.120), kind=kLoop, calls=%fused_computation.30 | loop fusion | flops 8355840 | bytes 7864324 | tf_op jit(solution)/shard_map/convert.2
  277.8 3.0 pad_maximum_fusion
  280.8 28.7 %all-gather.3.cloned.1.call-done = bf16[16,2,40,768]{3,2,0,1:T(8,128)(2,1)} async-done(((bf16[8,2,40,768]{3,2,0,1:T(8,128)(2,1)}), bf16[16,2,40,768]{3,2,0,1:T(8,128)(2,1)}) %all-gather.3.cloned.1.call-update) | async-done | bytes 1966096 | tf_op jit(solution)/shard_map/all_gather | solution.py:87
  309.5 3.8 convert_bitcast_fusion.1
  315.1 6.5 %all-to-all-start.1 = ((bf16[16,2,40,1024]{3,2,1,0:T(8,128)(2,1)}), bf16[16,2,40,1024]{3,2,1,0:T(8,128)(2,1)}, u32[]{:S(2)}, u32[]{:S(2)}) async-start(bf16[16,2,40,1024]{3,2,1,0:T(8,128)(2,1)} %copy.29), calls=%async_computation.1 | async-start | bytes 5242880 | tf_op jit(solution)/shard_map/all_to_all | solution.py:91
  321.6 43.1 %all-gather.5.cloned.1.call-done = bf16[16,2,40,1536]{3,2,0,1:T(8,128)(2,1)} async-done(((bf16[8,2,40,1536]{3,2,0,1:T(8,128)(2,1)}), bf16[16,2,40,1536]{3,2,0,1:T(8,128)(2,1)}) %all-gather.5.cloned.1.call-update) | async-done | bytes 3932176 | tf_op jit(solution)/shard_map/all_gather | solution.py:108
  364.7 8.3 %convert_bitcast_fusion = bf16[16,2,40,1024]{3,2,0,1:T(8,128)(2,1)S(1)} fusion(bf16[16,2,40,1536]{3,2,0,1:T(8,128)(2,1)} %all-gather.5.cloned.1.call-done, bf16[2,1024,768]{2,1,0:T(8,128)(2,1)} %param.11, bf16[2,1024,768]{2,1,0:T(8,128)(2,1)} %param.10), kind=kOutput, calls=%fused_computation.20 | convolution fusion | flops 4040425472 | bytes 12845056 | tf_op jit(solution)/shard_map/secf,edf->secd/dot_general | solution.py:109
  374.8 5.5 %all-to-all-done.1 = bf16[16,2,40,1024]{3,2,1,0:T(8,128)(2,1)} async-done(((bf16[16,2,40,1024]{3,2,1,0:T(8,128)(2,1)}), bf16[16,2,40,1024]{3,2,1,0:T(8,128)(2,1)}, u32[]{:S(2)}, u32[]{:S(2)}) %all-to-all-start.1) | async-done | bytes 2621472 | tf_op jit(solution)/shard_map/all_to_all | solution.py:91
  380.4 4.8 %all-to-all-start.2 = ((bf16[16,2,40,1024]{3,2,1,0:T(8,128)(2,1)}), bf16[16,2,40,1024]{3,2,1,0:T(8,128)(2,1)}, u32[]{:S(2)}, u32[]{:S(2)}) async-start(bf16[16,2,40,1024]{3,2,1,0:T(8,128)(2,1)} %copy.31), calls=%async_computation.2 | async-start | bytes 5242880 | tf_op jit(solution)/shard_map/all_to_all | solution.py:112
  385.3 8.1 %gather_fusion.1 = bf16[1024,1024]{1,0:T(8,128)(2,1)} fusion(bf16[1280,1024]{1,0:T(8,128)(2,1)} %bitcast.11, s32[1024]{0:T(1024)S(1)} %broadcast_clamp_fusion), kind=kCustom, calls=%fused_computation.1 | custom fusion | bytes 4198400 | tf_op jit(solution)/shard_map/gather | solution.py:57
  393.4 50.5 %all-to-all-done.2 = bf16[16,2,40,1024]{3,2,1,0:T(8,128)(2,1)} async-done(((bf16[16,2,40,1024]{3,2,1,0:T(8,128)(2,1)}), bf16[16,2,40,1024]{3,2,1,0:T(8,128)(2,1)}, u32[]{:S(2)}, u32[]{:S(2)}) %all-to-all-start.2) | async-done | bytes 2621472 | tf_op jit(solution)/shard_map/all_to_all | solution.py:112
  443.9 8.1 %gather_fusion.4 = bf16[1024,1024]{1,0:T(8,128)(2,1)} fusion(bf16[1280,1024]{1,0:T(8,128)(2,1)} %bitcast.50, s32[1024]{0:T(1024)S(1)} %broadcast_clamp_fusion), kind=kCustom, calls=%fused_computation.4 | custom fusion | bytes 4198400 | tf_op jit(solution)/shard_map/gather | solution.py:57
  452.0 6.7 %fusion = (bf16[128,1024]{1,0:T(8,128)(2,1)}, bf16[128,1024]{1,0:T(8,128)(2,1)}) fusion(bf16[1024,1024]{1,0:T(8,128)(2,1)} %gather_fusion.4, f32[128,8]{1,0:T(8,128)S(1)} %copy.22, bf16[1024,1024]{1,0:T(8,128)(2,1)} %gather_fusion.1), kind=kLoop, calls=%fused_computation.8 | loop fusion | flops 6029312 | bytes 4722688 | tf_op jit(solution)/shard_map/reduce_sum | solution.py:58
  (86 shorter events, 49.4 us)
Async XLA Ops:
  7.2 200.6 %copy-start = (bf16[2,768,1024]{2,1,0:T(8,128)(2,1)S(1)}, bf16[2,768,1024]{2,1,0:T(8,128)(2,1)}, u32[]{:S(2)}) copy-start(bf16[2,768,1024]{2,1,0:T(8,128)(2,1)} %param.12) | copy-start | bytes 9437188
  7.2 28.8 %copy-start.1 = (bf16[128,1024]{1,0:T(8,128)(2,1)S(1)}, bf16[128,1024]{1,0:T(8,128)(2,1)}, u32[]{:S(2)}) copy-start(bf16[128,1024]{1,0:T(8,128)(2,1)} %param.7) | copy-start | bytes 786436
  7.2 206.0 %reduce-scatter.5.cloned.1.call-start = ((), (), s32[]{:S(2)}) async-start(), calls=%async_computation.7 | async-start | bytes 5898240
  124.3 0.9 copy-start.2
  124.4 148.2 %all-reduce.2.cloned.1.call-start = ((), (), s32[]{:S(2)}) async-start(), calls=%async_computation.5 | async-start | bytes 3932160 | tf_op jit(solution)/shard_map/psum | solution.py:101
  134.1 3.7 collective-permute-start
  134.2 5.5 %collective-permute-start.1 = (bf16[1,2,40,1024]{3,2,1,0:T(8,128)(2,1)S(1)}, bf16[1,2,40,1024]{3,2,1,0:T(8,128)(2,1)S(1)}, u32[]{:S(2)}, u32[]{:S(2)}) collective-permute-start(bf16[1,2,40,1024]{3,2,1,0:T(8,128)(2,1)S(1)} %get-tuple-element.20), channel_id=1, source_target_pairs={{0,2},{1,3},{2,0},{3,1},{4,6},{5,7},{6,4},{7,5},{8,10},{9,11},{10,... | collective-permute-start | bytes 491528 | tf_op jit(solution)/shard_map/ppermute | solution.py:97
  134.7 9.3 %collective-permute-start.2 = (bf16[1,2,40,1024]{3,2,1,0:T(8,128)(2,1)S(1)}, bf16[1,2,40,1024]{3,2,1,0:T(8,128)(2,1)S(1)}, u32[]{:S(2)}, u32[]{:S(2)}) collective-permute-start(bf16[1,2,40,1024]{3,2,1,0:T(8,128)(2,1)S(1)} %get-tuple-element.19), channel_id=1, source_target_pairs={{0,3},{1,2},{2,1},{3,0},{4,7},{5,6},{6,5},{7,4},{8,11},{9,10},{10,... | collective-permute-start | bytes 491528 | tf_op jit(solution)/shard_map/ppermute | solution.py:97
  136.2 9.6 %collective-permute-start.3 = (bf16[1,2,40,1024]{3,2,1,0:T(8,128)(2,1)S(1)}, bf16[1,2,40,1024]{3,2,1,0:T(8,128)(2,1)S(1)}, u32[]{:S(2)}, u32[]{:S(2)}) collective-permute-start(bf16[1,2,40,1024]{3,2,1,0:T(8,128)(2,1)S(1)} %get-tuple-element.18), channel_id=1, source_target_pairs={{0,4},{1,5},{2,6},{3,7},{4,0},{5,1},{6,2},{7,3},{8,12},{9,13},{10,... | collective-permute-start | bytes 491528 | tf_op jit(solution)/shard_map/ppermute | solution.py:97
  136.6 10.9 %collective-permute-start.4 = (bf16[1,2,40,1024]{3,2,1,0:T(8,128)(2,1)S(1)}, bf16[1,2,40,1024]{3,2,1,0:T(8,128)(2,1)S(1)}, u32[]{:S(2)}, u32[]{:S(2)}) collective-permute-start(bf16[1,2,40,1024]{3,2,1,0:T(8,128)(2,1)S(1)} %get-tuple-element.17), channel_id=1, source_target_pairs={{0,5},{1,4},{2,7},{3,6},{4,1},{5,0},{6,3},{7,2},{8,13},{9,12},{10,... | collective-permute-start | bytes 491528 | tf_op jit(solution)/shard_map/ppermute | solution.py:97
  137.8 16.0 %collective-permute-start.5 = (bf16[1,2,40,1024]{3,2,1,0:T(8,128)(2,1)S(1)}, bf16[1,2,40,1024]{3,2,1,0:T(8,128)(2,1)S(1)}, u32[]{:S(2)}, u32[]{:S(2)}) collective-permute-start(bf16[1,2,40,1024]{3,2,1,0:T(8,128)(2,1)S(1)} %get-tuple-element.16), channel_id=1, source_target_pairs={{0,6},{1,7},{2,4},{3,5},{4,2},{5,3},{6,0},{7,1},{8,14},{9,15},{10,... | collective-permute-start | bytes 491528 | tf_op jit(solution)/shard_map/ppermute | solution.py:97
  139.7 19.6 %collective-permute-start.6 = (bf16[1,2,40,1024]{3,2,1,0:T(8,128)(2,1)S(1)}, bf16[1,2,40,1024]{3,2,1,0:T(8,128)(2,1)S(1)}, u32[]{:S(2)}, u32[]{:S(2)}) collective-permute-start(bf16[1,2,40,1024]{3,2,1,0:T(8,128)(2,1)S(1)} %get-tuple-element.15), channel_id=1, source_target_pairs={{0,7},{1,6},{2,5},{3,4},{4,3},{5,2},{6,1},{7,0},{8,15},{9,14},{10,... | collective-permute-start | bytes 491528 | tf_op jit(solution)/shard_map/ppermute | solution.py:97
  144.1 16.0 %collective-permute-start.7 = (bf16[1,2,40,1024]{3,2,1,0:T(8,128)(2,1)S(1)}, bf16[1,2,40,1024]{3,2,1,0:T(8,128)(2,1)S(1)}, u32[]{:S(2)}, u32[]{:S(2)}) collective-permute-start(bf16[1,2,40,1024]{3,2,1,0:T(8,128)(2,1)S(1)} %get-tuple-element.14), channel_id=1, source_target_pairs={{0,8},{1,9},{2,10},{3,11},{4,12},{5,13},{6,14},{7,15},{8,0},{9,1},... | collective-permute-start | bytes 491528 | tf_op jit(solution)/shard_map/ppermute | solution.py:97
  145.9 27.8 %collective-permute-start.8 = (bf16[1,2,40,1024]{3,2,1,0:T(8,128)(2,1)S(1)}, bf16[1,2,40,1024]{3,2,1,0:T(8,128)(2,1)S(1)}, u32[]{:S(2)}, u32[]{:S(2)}) collective-permute-start(bf16[1,2,40,1024]{3,2,1,0:T(8,128)(2,1)S(1)} %get-tuple-element.13), channel_id=1, source_target_pairs={{0,9},{1,8},{2,11},{3,10},{4,13},{5,12},{6,15},{7,14},{8,1},{9,0},... | collective-permute-start | bytes 491528 | tf_op jit(solution)/shard_map/ppermute | solution.py:97
  147.4 33.3 %collective-permute-start.9 = (bf16[1,2,40,1024]{3,2,1,0:T(8,128)(2,1)S(1)}, bf16[1,2,40,1024]{3,2,1,0:T(8,128)(2,1)S(1)}, u32[]{:S(2)}, u32[]{:S(2)}) collective-permute-start(bf16[1,2,40,1024]{3,2,1,0:T(8,128)(2,1)S(1)} %get-tuple-element.12), channel_id=1, source_target_pairs={{0,10},{1,11},{2,8},{3,9},{4,14},{5,15},{6,12},{7,13},{8,2},{9,3},... | collective-permute-start | bytes 491528 | tf_op jit(solution)/shard_map/ppermute | solution.py:97
  153.8 32.3 %collective-permute-start.10 = (bf16[1,2,40,1024]{3,2,1,0:T(8,128)(2,1)S(1)}, bf16[1,2,40,1024]{3,2,1,0:T(8,128)(2,1)S(1)}, u32[]{:S(2)}, u32[]{:S(2)}) collective-permute-start(bf16[1,2,40,1024]{3,2,1,0:T(8,128)(2,1)S(1)} %get-tuple-element.11), channel_id=1, source_target_pairs={{0,11},{1,10},{2,9},{3,8},{4,15},{5,14},{6,13},{7,12},{8,3},{9,2},... | collective-permute-start | bytes 491528 | tf_op jit(solution)/shard_map/ppermute | solution.py:97
  159.3 32.7 %collective-permute-start.11 = (bf16[1,2,40,1024]{3,2,1,0:T(8,128)(2,1)S(1)}, bf16[1,2,40,1024]{3,2,1,0:T(8,128)(2,1)S(1)}, u32[]{:S(2)}, u32[]{:S(2)}) collective-permute-start(bf16[1,2,40,1024]{3,2,1,0:T(8,128)(2,1)S(1)} %get-tuple-element.10), channel_id=1, source_target_pairs={{0,12},{1,13},{2,14},{3,15},{4,8},{5,9},{6,10},{7,11},{8,4},{9,5},... | collective-permute-start | bytes 491528 | tf_op jit(solution)/shard_map/ppermute | solution.py:97
  160.1 35.4 %collective-permute-start.12 = (bf16[1,2,40,1024]{3,2,1,0:T(8,128)(2,1)S(1)}, bf16[1,2,40,1024]{3,2,1,0:T(8,128)(2,1)S(1)}, u32[]{:S(2)}, u32[]{:S(2)}) collective-permute-start(bf16[1,2,40,1024]{3,2,1,0:T(8,128)(2,1)S(1)} %get-tuple-element.9), channel_id=1, source_target_pairs={{0,13},{1,12},{2,15},{3,14},{4,9},{5,8},{6,11},{7,10},{8,5},{9,4},... | collective-permute-start | bytes 491528 | tf_op jit(solution)/shard_map/ppermute | solution.py:97
  173.7 25.9 %collective-permute-start.13 = (bf16[1,2,40,1024]{3,2,1,0:T(8,128)(2,1)S(1)}, bf16[1,2,40,1024]{3,2,1,0:T(8,128)(2,1)S(1)}, u32[]{:S(2)}, u32[]{:S(2)}) collective-permute-start(bf16[1,2,40,1024]{3,2,1,0:T(8,128)(2,1)S(1)} %get-tuple-element.8), channel_id=1, source_target_pairs={{0,14},{1,15},{2,12},{3,13},{4,10},{5,11},{6,8},{7,9},{8,6},{9,7},... | collective-permute-start | bytes 491528 | tf_op jit(solution)/shard_map/ppermute | solution.py:97
  180.7 22.4 %collective-permute-start.14 = (bf16[1,2,40,1024]{3,2,1,0:T(8,128)(2,1)S(1)}, bf16[1,2,40,1024]{3,2,1,0:T(8,128)(2,1)S(1)}, u32[]{:S(2)}, u32[]{:S(2)}) collective-permute-start(bf16[1,2,40,1024]{3,2,1,0:T(8,128)(2,1)S(1)} %get-tuple-element.7), channel_id=1, source_target_pairs={{0,15},{1,14},{2,13},{3,12},{4,11},{5,10},{6,9},{7,8},{8,7},{9,6},... | collective-permute-start | bytes 491528 | tf_op jit(solution)/shard_map/ppermute | solution.py:97
  213.1 96.4 %all-gather.3.cloned.1.call-start = ((), (), s32[]{:S(2)}) async-start(), calls=%async_computation.4 | async-start | bytes 2949120 | tf_op jit(solution)/shard_map/all_gather | solution.py:87
  277.7 87.0 %all-gather.5.cloned.1.call-start = ((), (), s32[]{:S(2)}) async-start(), calls=%async_computation.6 | async-start | bytes 5898240 | tf_op jit(solution)/shard_map/all_gather | solution.py:108
  315.1 65.3 %all-to-all-start.1 = ((bf16[16,2,40,1024]{3,2,1,0:T(8,128)(2,1)}), bf16[16,2,40,1024]{3,2,1,0:T(8,128)(2,1)}, u32[]{:S(2)}, u32[]{:S(2)}) async-start(bf16[16,2,40,1024]{3,2,1,0:T(8,128)(2,1)} %copy.29), calls=%async_computation.1 | async-start | bytes 5242880 | tf_op jit(solution)/shard_map/all_to_all | solution.py:91
  374.8 10.3 %copy-start.3 = (f32[128,8]{0,1:T(8,128)S(1)}, f32[128,8]{0,1:T(8,128)}, u32[]{:S(2)}) copy-start(f32[128,8]{0,1:T(8,128)} %param.9) | copy-start | bytes 12292
  380.4 63.5 %all-to-all-start.2 = ((bf16[16,2,40,1024]{3,2,1,0:T(8,128)(2,1)}), bf16[16,2,40,1024]{3,2,1,0:T(8,128)(2,1)}, u32[]{:S(2)}, u32[]{:S(2)}) async-start(bf16[16,2,40,1024]{3,2,1,0:T(8,128)(2,1)} %copy.31), calls=%async_computation.2 | async-start | bytes 5242880 | tf_op jit(solution)/shard_map/all_to_all | solution.py:112
Sparse Core Ops, SparseCore 0:
  124.5 51.6 reduce-scatter.4
  213.2 59.3 all-reduce.1
  277.9 31.6 all-gather.2
  310.9 53.7 all-gather.4
